TPU v7x, 32 devices: a whole 2x2x4 slice. The times are simulated.
32 devices in a mesh: chan: 4 (over x, core), az: 2 (over y), rng: 4 (over z).
Axes of the slice: x: 2, y: 2, z: 4, core: 2. Of those that a mesh axis runs over, the one named last changes fastest.
Arguments:
- raw: float32 [2, 16, 64, 16384], P(None, 'chan', 'rng', 'az'), may hold values from -6 to 6
- taps: float32 [2, 17, 64], P(None, None, 'rng'), may hold values from -1.5 to 1.5
- recon: float32 [2, 16, 16, 16384], P(None, 'az', None, ('chan', 'rng')), may hold values from -1 to 1
- channel_slot: int32 [16], replicated, may hold values from 0 to 15, each once
Outputs:
- reconstructed: float32 [2, 16, 4, 16, 16384], P(None, None, None, 'az', ('chan', 'rng'))
Inputs may be any that keep to these rules, and one draw needn't show every extreme that they name: `channel_slot`: a permutation of the channels.
All inputs are finite; a program needn't handle non-finite values.
Results may differ from a plain program's by a relative error of at most 0.0003.
Values sent between devices are 32-bit elements; how exact they have to be, the bound alone decides.
No kernel may reach another device: no remote copies, remote signals or barrier semaphores. Data moves between devices by JAX's collectives and lax.ppermute only.
A program may use at most 192 MiB of HBM per device.

v0:
```python
import math
import jax
import jax.numpy as jnp
from jax import lax
from jax.sharding import PartitionSpec as P


def with_halo(shard, sides, width):
    for axis, dim in sides:
        size, length = (lax.axis_size(axis), shard.shape[dim])
        up = [(i, (i + 1) % size) for i in range(size - 1)]
        down = [(j, i) for i, j in up]
        last = lax.slice_in_dim(shard, length - width, length, axis=dim)
        leading = lax.slice_in_dim(shard, 0, width, axis=dim)
        before = lax.ppermute(last, axis, up)
        after = lax.ppermute(leading, axis, down)
        shard = jnp.concatenate([before, shard, after], axis=dim)
    return shard


def phases(first, second, length):
    left = jnp.arange(first, dtype=jnp.int32)
    right = jnp.arange(second, dtype=jnp.int32)
    product = left[:, None] * right[None, :] % length
    angle = product.astype(jnp.float32) * (2.0 * math.pi / length)
    return (jnp.cos(angle), jnp.sin(angle))


def azimuth_fft(block):
    count = block.shape[-1]
    rows = math.isqrt(count)
    while count % rows:
        rows = rows - 1
    cols = count // rows
    lead = block.shape[1:-1]
    high = lax.Precision.HIGHEST
    real_in = block[0].reshape(lead + (rows, cols))
    imag_in = block[1].reshape(lead + (rows, cols))
    cosine_first, sine_first = phases(rows, rows, rows)
    first_real = jnp.einsum("...ab,af->...bf", real_in, cosine_first, precision=high) + jnp.einsum(
        "...ab,af->...bf", imag_in, sine_first, precision=high
    )
    first_imag = jnp.einsum("...ab,af->...bf", imag_in, cosine_first, precision=high) - jnp.einsum(
        "...ab,af->...bf", real_in, sine_first, precision=high
    )
    twist_cos, twist_sin = phases(cols, rows, count)
    turned_real = first_real * twist_cos + first_imag * twist_sin
    turned_imag = first_imag * twist_cos - first_real * twist_sin
    cosine_second, sine_second = phases(cols, cols, cols)
    out_real = jnp.einsum(
        "...bf,bg->...gf", turned_real, cosine_second, precision=high
    ) + jnp.einsum("...bf,bg->...gf", turned_imag, sine_second, precision=high)
    out_imag = jnp.einsum(
        "...bf,bg->...gf", turned_imag, cosine_second, precision=high
    ) - jnp.einsum("...bf,bg->...gf", turned_real, sine_second, precision=high)
    scale = 1.0 / math.sqrt(count)
    return jnp.stack([out_real.reshape(lead + (count,)), out_imag.reshape(lead + (count,))]) * scale


def shards(raw, taps, recon, channel_slot):
    width = taps.shape[1]
    half = (width - 1) // 2
    strip_rows = raw.shape[2]
    padded = with_halo(raw, (("rng", 2),), half)
    real_part = jnp.zeros(raw.shape[1:], jnp.float32)
    imag_part = jnp.zeros(raw.shape[1:], jnp.float32)
    for offset in range(width):
        seg_real = padded[0, :, offset : offset + strip_rows, :]
        seg_imag = padded[1, :, offset : offset + strip_rows, :]
        tap_real = taps[0, offset][None, :, None]
        tap_imag = taps[1, offset][None, :, None]
        real_part = real_part + tap_real * seg_real - tap_imag * seg_imag
        imag_part = imag_part + tap_real * seg_imag + tap_imag * seg_real
    filtered = jnp.stack([real_part, imag_part])
    spectrum = azimuth_fft(lax.all_to_all(filtered, "az", split_axis=2, concat_axis=3, tiled=True))
    strips = lax.axis_size("rng")
    groups = lax.axis_size("chan")
    local_channels = spectrum.shape[1]
    local_range = spectrum.shape[2]
    moved = lax.all_to_all(
        spectrum[:, None], ("chan", "rng"), split_axis=4, concat_axis=1, tiled=True
    )
    bins = moved.shape[-1]
    moved = moved.reshape((2, groups, strips, local_channels, local_range, bins))
    doppler = jnp.transpose(moved, (0, 1, 3, 2, 4, 5)).reshape(
        (2, groups * local_channels, strips * local_range, bins)
    )
    channels = doppler.shape[1]
    selector = (channel_slot[:, None] == jnp.arange(channels, dtype=jnp.int32)[None, :]).astype(
        jnp.float32
    )
    piece = lax.all_gather(recon, "az", axis=1, tiled=True)
    arranged = jnp.einsum("pkjf,cj->pkcf", piece, selector, precision=lax.Precision.HIGHEST)
    shape = (piece.shape[1], doppler.shape[2], doppler.shape[3])
    out_real = jnp.zeros(shape, jnp.float32)
    out_imag = jnp.zeros(shape, jnp.float32)
    for channel in range(channels):
        mat_real = arranged[0, :, channel, None, :]
        mat_imag = arranged[1, :, channel, None, :]
        data_real = doppler[0, channel][None]
        data_imag = doppler[1, channel][None]
        out_real = out_real + mat_real * data_real - mat_imag * data_imag
        out_imag = out_imag + mat_real * data_imag + mat_imag * data_real
    result = jnp.stack([out_real, out_imag])
    total_range = result.shape[2]
    return result.reshape((2, result.shape[1], strips, total_range // strips, result.shape[3]))


def solution(mesh):
    return jax.shard_map(
        shards,
        mesh=mesh,
        in_specs=(
            P(None, "chan", "rng", "az"),
            P(None, None, "rng"),
            P(None, "az", None, ("chan", "rng")),
            P(),
        ),
        out_specs=P(None, None, None, "az", ("chan", "rng")),
        check_vma=False,
    )
```

profile of v0, /device:TPU:0, one launch (start us, length us, event | category | flops | bytes accessed | tf_op | source)
XLA Modules:
  0.0 701.0 jit_solution(1237962557530691339)
XLA Ops:
  6.5 2.5 fusion.71
  9.0 5.1 collective-permute-start
  14.1 1.3 collective-permute-start.1
  15.5 0.5 slice_reduce_fusion.33
  15.9 0.4 slice_reduce_fusion.32
  16.4 42.5 %collective-permute-done = f32[2,4,8,8192]{3,2,1,0:T(8,128)S(1)} collective-permute-done((f32[2,4,8,8192]{3,2,1,0:T(8,128)S(1)}, f32[2,4,8,8192]{3,2,1,0:T(8,128)S(1)}, u32[]{:S(2)}, u32[]{:S(2)}) %collective-permute-start) | collective-permute-done | bytes 2097184 | tf_op jit(solution)/shard_map/ppermute | solution.py:15
  58.9 1.5 constant_dynamic-update-slice_fusion.1
  60.4 4.2 constant_dynamic-update-slice_fusion
  64.6 1.5 constant_dynamic-update-slice_fusion.2
  66.1 44.7 %multiply_subtract_fusion.2 = f32[1,4,16,8192]{3,2,1,0:T(8,128)} fusion(f32[2,4,24,8192]{3,2,1,0:T(8,128)} %constant_dynamic-update-slice_fusion.2, f32[2,4,24,8192]{3,2,1,0:T(8,128)} %get-tuple-element.73, f32[2,4,16,8192]{3,2,1,0:T(8,128)S(1)} %copy-done, f32[16]{0:T(128)S(1)} %get-tuple-element.37, f32[16]{0:T(128)S(1)} %get-tuple-element.38, ...), kind=kLoop, calls=%fused_computation.11 | loop fusion | flops 35127296 | bytes 73402496 | tf_op jit(solution)/shard_map/sub | solution.py:72
  110.8 44.8 %multiply_add_fusion.2 = f32[1,4,16,8192]{3,2,1,0:T(8,128)} fusion(f32[2,4,24,8192]{3,2,1,0:T(8,128)} %constant_dynamic-update-slice_fusion.2, f32[2,4,24,8192]{3,2,1,0:T(8,128)} %get-tuple-element.73, f32[2,4,16,8192]{3,2,1,0:T(8,128)S(1)} %copy-done, f32[16]{0:T(128)S(1)} %get-tuple-element.37, f32[16]{0:T(128)S(1)} %get-tuple-element.38, ...), kind=kLoop, calls=%fused_computation.10 | loop fusion | flops 35127296 | bytes 73402496 | tf_op jit(solution)/shard_map/add | solution.py:73
  155.5 2.5 pad_maximum_fusion
  158.1 4.7 copy.126
  162.8 5.8 all-to-all-start
  168.9 0.3 fusion.23
  169.3 46.1 %all-to-all-done = f32[2,4,16,8192]{3,1,0,2:T(4,128)} async-done(((f32[2,4,16,8192]{3,1,0,2:T(4,128)}), f32[2,4,16,8192]{3,1,0,2:T(4,128)}, u32[]{:S(2)}, u32[]{:S(2)}) %all-to-all-start) | async-done | bytes 4194336 | tf_op jit(solution)/shard_map/all_to_all | solution.py:75
  215.4 5.4 copy.224
  220.8 2.3 fusion.70
  223.1 3.1 reshape_squeeze.7
  226.1 4.9 fusion.6
  231.0 4.2 reshape_squeeze.6
  235.2 5.4 fusion.8
  240.6 3.7 convolution_subtract_fusion
  244.3 3.6 convolution_add_fusion
  247.9 2.7 fusion
  250.6 3.5 fusion.1
  254.1 3.7 add_bitcast_fusion
  257.8 2.7 stack.18
  260.5 5.8 subtract_bitcast_fusion
  266.3 2.9 stack.19
  269.2 3.9 maximum_multiply_fusion
  273.1 44.6 %copy.138 = f32[2,1,4,8,16384]{3,2,1,0,4:T(4,128)} copy(f32[2,1,4,8,16384]{4,3,2,1,0:T(8,128)} %maximum_multiply_fusion) | data formatting | bytes 8388608 | tf_op jit(solution)/shard_map/mul | solution.py:57
  317.7 82.5 %reshape.729 = f32[16,1,65536]{2,1,0:T(1,128)} reshape(f32[16384,2,1,4,8]{4,3,2,1,0:T(4,128)} %bitcast.180) | data formatting | bytes 8388608
  400.3 7.0 all-to-all-start.1
  407.3 0.7 all-gather.2.cloned.1.call-update
  408.0 35.1 %all-gather.2.cloned.1.call-done = f32[2,16,16,1024]{3,2,1,0:T(8,128)} async-done(((f32[2,8,16,1024]{3,2,1,0:T(8,128)}), f32[2,16,16,1024]{3,2,1,0:T(8,128)}) %all-gather.2.cloned.1.call-update) | async-done | bytes 2097168 | tf_op jit(solution)/shard_map/all_gather | solution.py:92
  443.1 2.7 convolution_bitcast_fusion
  445.8 1.1 fusion.72
  447.2 0.8 fusion.73
  448.2 53.3 %all-to-all-done.1 = f32[16,1,65536]{2,1,0:T(1,128)} async-done(((f32[16,1,65536]{2,1,0:T(1,128)}), f32[16,1,65536]{2,1,0:T(1,128)}, u32[]{:S(2)}, u32[]{:S(2)}) %all-to-all-start.1) | async-done | bytes 4194336 | tf_op jit(solution)/shard_map/all_to_all | solution.py:80
  501.6 0.5 broadcast.1262
  502.1 13.7 %reduce.68 = f32[16,65536]{1,0:T(8,128)} reduce(f32[16,1,65536]{2,1,0:T(1,128)} %all-to-all-done.1, f32[]{:T(128)} %broadcast.1262), dimensions={1}, to_apply=%all_to_all.25.reduce_sub_computation | reduce | bytes 8388612 | tf_op jit(solution)/shard_map/all_to_all | solution.py:80
  515.8 109.0 %reshape.730 = f32[16384,2,1,4,8]{4,3,2,1,0:T(4,128)} reshape(f32[16,65536]{1,0:T(8,128)} %reduce.68) | data formatting | bytes 8388608
  624.8 53.3 %copy.158 = f32[2,1,4,8,16,1024]{5,3,2,4,0,1:T(8,128)} copy(f32[2,1,4,8,16,1024]{3,2,0,5,4,1:T(4,128)} %bitcast.17) | data formatting | bytes 8388608 | tf_op jit(solution)/shard_map/all_to_all | solution.py:80
  678.1 2.5 copy.141
  681.0 5.3 multiply_subtract_fusion
  686.3 5.3 multiply_add_fusion
  691.7 2.3 pad_maximum_fusion.1
  (41 shorter events, 1.3 us)
Async XLA Ops:
  6.5 8.9 %copy-start.7 = (f32[2,17,16]{1,2,0:T(8,128)S(1)}, f32[2,17,16]{1,2,0:T(8,128)}, u32[]{:S(2)}) copy-start(f32[2,17,16]{1,2,0:T(8,128)} %param.5) | copy-start | bytes 6532
  9.0 49.8 %collective-permute-start = (f32[2,4,8,8192]{3,2,1,0:T(8,128)S(1)}, f32[2,4,8,8192]{3,2,1,0:T(8,128)S(1)}, u32[]{:S(2)}, u32[]{:S(2)}) collective-permute-start(f32[2,4,8,8192]{3,2,1,0:T(8,128)S(1)} %get-tuple-element.75), channel_id=1, source_target_pairs={{0,1},{1,2},{2,3},{4,5},{5,6},{6,7},{8,9},{9,10},{10,11},{12,13},{... | collective-permute-start | bytes 6291464 | tf_op jit(solution)/shard_map/ppermute | solution.py:15
  14.1 50.5 %collective-permute-start.1 = (f32[2,4,8,8192]{3,2,1,0:T(8,128)S(1)}, f32[2,4,8,8192]{3,2,1,0:T(8,128)S(1)}, u32[]{:S(2)}, u32[]{:S(2)}) collective-permute-start(f32[2,4,8,8192]{3,2,1,0:T(8,128)S(1)} %get-tuple-element.76), channel_id=1, source_target_pairs={{1,0},{2,1},{3,2},{5,4},{6,5},{7,6},{9,8},{10,9},{11,10},{13,12},{... | collective-permute-start | bytes 6291464 | tf_op jit(solution)/shard_map/ppermute | solution.py:16
  16.4 44.0 %copy-start = (f32[2,4,16,8192]{3,2,1,0:T(8,128)S(1)}, f32[2,4,16,8192]{3,2,1,0:T(8,128)}, u32[]{:S(2)}) copy-start(f32[2,4,16,8192]{3,2,1,0:T(8,128)} %param.4) | copy-start | bytes 12582916
  162.8 52.6 %all-to-all-start = ((f32[2,4,16,8192]{3,1,0,2:T(4,128)}), f32[2,4,16,8192]{3,1,0,2:T(4,128)}, u32[]{:S(2)}, u32[]{:S(2)}) async-start(f32[2,4,16,8192]{3,1,0,2:T(4,128)} %copy.126), calls=%async_computation | async-start | bytes 8388608 | tf_op jit(solution)/shard_map/all_to_all | solution.py:75
  226.1 4.9 copy-start.2
  235.2 5.4 copy-start.4
  235.2 5.4 copy-start.5
  240.6 3.7 copy-start.3
  247.9 6.2 copy-start.1
  266.3 2.9 copy-start.6
  400.3 42.8 %copy-start.8 = (s32[16]{0:T(128)S(1)}, s32[16]{0:T(128)}, u32[]{:S(2)}) copy-start(s32[16]{0:T(128)} %param.7) | copy-start | bytes 196
  400.3 101.3 %all-to-all-start.1 = ((f32[16,1,65536]{2,1,0:T(1,128)}), f32[16,1,65536]{2,1,0:T(1,128)}, u32[]{:S(2)}, u32[]{:S(2)}) async-start(f32[16,1,65536]{2,1,0:T(1,128)} %reshape.729), calls=%async_computation.1 | async-start | bytes 8388608 | tf_op jit(solution)/shard_map/all_to_all | solution.py:80
  407.3 35.8 %all-gather.2.cloned.1.call-start = ((), (), s32[]{:S(2)}) async-start(), calls=%async_computation.2 | async-start | bytes 3145728 | tf_op jit(solution)/shard_map/all_gather | solution.py:92
Sparse Core Ops, SparseCore 0:
  409.6 33.4 all-gather.1
where the time goes:
time: 714 us; the launch traced here: 701 us
  local copies, waits for them, and re-layouts  331 us (46%)
  waiting for transfers between devices  178 us (25%)
  other arithmetic  123 us (17%)
  matrix products  35.9 us (5%)
  starting transfers between devices  19.2 us (3%)
  between operations  14 us (2%)
    unnamed x37, local copies, waits for them, and re-layouts  193 us
    all_to_all x2, local copies, waits for them, and re-layouts, shards(): lax.all_to_all(spectrum[:, None], ('chan', 'rng'), split_axis=4, concat_a...  53.9 us
    all_to_all x1, waiting for transfers between devices, shards(): lax.all_to_all(spectrum[:, None], ('chan', 'rng'), split_axis=4, concat_a...  53.3 us
    all_to_all x1, waiting for transfers between devices, shards(): lax.all_to_all(filtered, 'az', split_axis=2, concat_axis=3, tiled=True)  46.1 us
    add x1, other arithmetic, shards(): imag_part = imag_part + tap_real * seg_imag + tap_imag * seg_real  44.8 us
    sub x1, other arithmetic, shards(): real_part = real_part + tap_real * seg_real - tap_imag * seg_imag  44.7 us
    mul x1, local copies, waits for them, and re-layouts, azimuth_fft(): jnp.stack([out_real.reshape(lead + (count,)), out_imag.reshape(lead + (co...  44.6 us
    ppermute x1, waiting for transfers between devices, with_halo(): before = lax.ppermute(last, axis, up)  42.5 us
  transfers between devices with their start and end apart: 5, of which 4 were waited for; matrix products, arithmetic and copies ran while one was open for 2% of the time, Pallas kernels for 0%

commit v1 on v0

--- a/solution.py
+++ b/solution.py
@@ -3,6 +3,28 @@
 import jax.numpy as jnp
 from jax import lax
 from jax.sharding import PartitionSpec as P
+
+
+def in_blocks(value, dim, size):
+    before, after = (value.shape[:dim], value.shape[dim + 1 :])
+    return jnp.moveaxis(value.reshape(*before, size, -1, *after), dim, 0)
+
+
+def laid_out(pieces, dim):
+    pieces = jnp.moveaxis(pieces, 0, dim)
+    lengths = pieces.shape
+    return pieces.reshape(*lengths[:dim], lengths[dim] * lengths[dim + 1], *lengths[dim + 2 :])
+
+
+def exchange_in_pairs(x, axis, split_dim, concat_dim):
+    size, index = (lax.axis_size(axis), lax.axis_index(axis))
+    tiles = in_blocks(x, split_dim, size)
+    gathered = [tiles[index]]
+    for step in range(1, size):
+        sent = tiles[index ^ step]
+        gathered.append(lax.ppermute(sent, axis, [(i, i ^ step) for i in range(size)]))
+    tiles = jnp.stack(gathered)[index ^ jnp.arange(size)]
+    return laid_out(tiles, concat_dim)
 
 
 def with_halo(shard, sides, width):
@@ -77,9 +99,7 @@
     groups = lax.axis_size("chan")
     local_channels = spectrum.shape[1]
     local_range = spectrum.shape[2]
-    moved = lax.all_to_all(
-        spectrum[:, None], ("chan", "rng"), split_axis=4, concat_axis=1, tiled=True
-    )
+    moved = exchange_in_pairs(spectrum[:, None], ("chan", "rng"), 4, 1)
     bins = moved.shape[-1]
     moved = moved.reshape((2, groups, strips, local_channels, local_range, bins))
     doppler = jnp.transpose(moved, (0, 1, 3, 2, 4, 5)).reshape(

time: 714 us -> 409 us (0.57)
  local copies, waits for them, and re-layouts: 331 us -> 75.2 us
  waiting for transfers between devices: 178 us -> 112 us
  starting transfers between devices: 19.2 us -> 56.8 us
  other arithmetic: 123 us -> 108 us
    unnamed x37 -> x91, local copies, waits for them, and re-layouts: 193 us -> 21.2 us
    all_to_all x2 -> x0, local copies, waits for them, and re-layouts: 53.9 us -> none  [shards(): lax.all_to_all(spectrum[:, None], ('chan', 'rng'), split_axis=4, concat_a...]
    all_to_all x1 -> x0, waiting for transfers between devices: 53.3 us -> none  [shards(): lax.all_to_all(spectrum[:, None], ('chan', 'rng'), split_axis=4, concat_a...]
    mul x1 -> x0, local copies, waits for them, and re-layouts: 44.6 us -> none  [azimuth_fft(): jnp.stack([out_real.reshape(lead + (count,)), out_imag.reshape(lead + (co...]
    ppermute x0 -> x15, starting transfers between devices: none -> 43.3 us  [exchange_in_pairs(): lax.ppermute(sent, axis, [(i, i ^ step) for i in range(size)])]
    all_gather x1, waiting for transfers between devices: 35.1 us -> 0.02 us  [shards(): piece = lax.all_gather(recon, 'az', axis=1, tiled=True)]
    ppermute x0 -> x15, waiting for transfers between devices: none -> 34.4 us  [exchange_in_pairs(): lax.ppermute(sent, axis, [(i, i ^ step) for i in range(size)])]
    all_to_all x1 -> x0, other arithmetic: 13.7 us -> none  [shards(): lax.all_to_all(spectrum[:, None], ('chan', 'rng'), split_axis=4, concat_a...]
  transfers between devices with their start and end apart: 5 -> 19, of which waited for: 4 -> 8; matrix products, arithmetic and copies ran while one was open for 2% -> 32% of each run, Pallas kernels for 0% -> 0%
where the time goes in v1:
time: 409 us; the launch traced here: 402 us
  waiting for transfers between devices  112 us (27%)
  other arithmetic  108 us (26%)
  local copies, waits for them, and re-layouts  75.2 us (18%)
  starting transfers between devices  56.8 us (14%)
  matrix products  35.6 us (9%)
  between operations  14.4 us (4%)
    add x1, other arithmetic, shards(): imag_part = imag_part + tap_real * seg_imag + tap_imag * seg_real  44.9 us
    sub x1, other arithmetic, shards(): real_part = real_part + tap_real * seg_real - tap_imag * seg_imag  44.8 us
    ppermute x15, starting transfers between devices, exchange_in_pairs(): lax.ppermute(sent, axis, [(i, i ^ step) for i in range(size)])  43.3 us
    ppermute x1, waiting for transfers between devices, with_halo(): before = lax.ppermute(last, axis, up)  40.7 us
    all_to_all x1, waiting for transfers between devices, shards(): lax.all_to_all(filtered, 'az', split_axis=2, concat_axis=3, tiled=True)  36.9 us
    ppermute x15, waiting for transfers between devices, exchange_in_pairs(): lax.ppermute(sent, axis, [(i, i ^ step) for i in range(size)])  34.4 us
    unnamed x91, local copies, waits for them, and re-layouts  21.2 us
  transfers between devices with their start and end apart: 19, of which 8 were waited for; matrix products, arithmetic and copies ran while one was open for 32% of the time, Pallas kernels for 0%

profile of v1, /device:TPU:0, one launch (start us, length us, event | category | flops | bytes accessed | tf_op | source)
XLA Modules:
  0.0 401.7 jit_solution(14900316004528743159)
XLA Ops:
  6.5 4.7 %fusion.72 = (f32[2,4,8,8192]{3,2,1,0:T(8,128)}, f32[2,4,8,8192]{3,2,1,0:T(8,128)}) fusion(f32[2,4,16,8192]{3,2,1,0:T(8,128)} %param.4), kind=kLoop, calls=%fused_computation.237 | loop fusion | bytes 8388608 | tf_op jit(solution)/shard_map/slice | solution.py:35
  11.2 6.3 %collective-permute-start = (f32[2,4,8,8192]{3,2,1,0:T(8,128)}, f32[2,4,8,8192]{3,2,1,0:T(8,128)}, u32[]{:S(2)}, u32[]{:S(2)}) collective-permute-start(f32[2,4,8,8192]{3,2,1,0:T(8,128)} %get-tuple-element.91), channel_id=1, source_target_pairs={{0,1},{1,2},{2,3},{4,5},{5,6},{6,7},{8,9},{9,10},{10,11},{12,13},{... | collective-permute-start | bytes 6291464 | tf_op jit(solution)/shard_map/ppermute | solution.py:37
  17.5 1.3 collective-permute-start.1
  20.6 40.7 %collective-permute-done = f32[2,4,8,8192]{3,2,1,0:T(8,128)} collective-permute-done((f32[2,4,8,8192]{3,2,1,0:T(8,128)}, f32[2,4,8,8192]{3,2,1,0:T(8,128)}, u32[]{:S(2)}, u32[]{:S(2)}) %collective-permute-start) | collective-permute-done | bytes 2097184 | tf_op jit(solution)/shard_map/ppermute | solution.py:37
  61.3 3.1 constant_dynamic-update-slice_fusion.1
  64.4 4.2 %constant_dynamic-update-slice_fusion = (f32[2,4,24,8192]{3,2,1,0:T(8,128)}, f32[2,4,24,8192]{3,2,1,0:T(8,128)}) fusion(f32[2,4,24,8192]{3,2,1,0:T(8,128)} %constant_dynamic-update-slice_fusion.1, f32[2,4,16,8192]{3,2,1,0:T(8,128)S(1)} %copy-done), kind=kLoop, calls=%fused_computation.140 | loop fusion | bytes 12582912 | tf_op jit(solution)/shard_map/concatenate | solution.py:39
  68.6 3.0 constant_dynamic-update-slice_fusion.2
  71.7 44.9 %multiply_add_fusion.2 = f32[1,4,16,8192]{3,2,1,0:T(8,128)} fusion(f32[2,4,24,8192]{3,2,1,0:T(8,128)} %constant_dynamic-update-slice_fusion.2, f32[2,4,24,8192]{3,2,1,0:T(8,128)} %get-tuple-element.89, f32[2,4,16,8192]{3,2,1,0:T(8,128)S(1)} %copy-done, f32[16]{0:T(128)S(1)} %get-tuple-element.37, f32[16]{0:T(128)S(1)} %get-tuple-element.38, ...), kind=kLoop, calls=%fused_computation.11 | loop fusion | flops 35127296 | bytes 73402496 | tf_op jit(solution)/shard_map/add | solution.py:95
  116.6 44.8 %multiply_subtract_fusion.2 = f32[1,4,16,8192]{3,2,1,0:T(8,128)} fusion(f32[2,4,24,8192]{3,2,1,0:T(8,128)} %constant_dynamic-update-slice_fusion.2, f32[2,4,24,8192]{3,2,1,0:T(8,128)} %get-tuple-element.89, f32[2,4,16,8192]{3,2,1,0:T(8,128)S(1)} %copy-done, f32[16]{0:T(128)S(1)} %get-tuple-element.37, f32[16]{0:T(128)S(1)} %get-tuple-element.38, ...), kind=kLoop, calls=%fused_computation.12 | loop fusion | flops 35127296 | bytes 73402496 | tf_op jit(solution)/shard_map/sub | solution.py:94
  161.4 2.5 pad_maximum_fusion
  163.9 4.7 %copy.73 = f32[2,4,16,8192]{3,1,0,2:T(4,128)} copy(f32[2,4,16,8192]{3,2,1,0:T(8,128)S(1)} %pad_maximum_fusion) | data formatting | bytes 8388608 | tf_op jit(solution)/shard_map/stack | solution.py:96
  168.6 6.0 %all-to-all-start = ((f32[2,4,16,8192]{3,1,0,2:T(4,128)}), f32[2,4,16,8192]{3,1,0,2:T(4,128)}, u32[]{:S(2)}, u32[]{:S(2)}) async-start(f32[2,4,16,8192]{3,1,0,2:T(4,128)} %copy.73), calls=%async_computation | async-start | bytes 8388608 | tf_op jit(solution)/shard_map/all_to_all | solution.py:97
  174.6 2.7 convolution_bitcast_fusion
  177.4 1.5 fusion.73
  184.4 36.9 %all-to-all-done = f32[2,4,16,8192]{3,1,0,2:T(4,128)} async-done(((f32[2,4,16,8192]{3,1,0,2:T(4,128)}), f32[2,4,16,8192]{3,1,0,2:T(4,128)}, u32[]{:S(2)}, u32[]{:S(2)}) %all-to-all-start) | async-done | bytes 4194336 | tf_op jit(solution)/shard_map/all_to_all | solution.py:97
  221.4 5.4 %copy.200 = f32[2,4,2,8,8192]{4,2,3,1,0:T(2,128)S(1)} copy(f32[2,4,2,8,8192]{4,1,0,3,2:T(4,128)} %bitcast.5) | data formatting | bytes 8388608 | tf_op jit(solution)/shard_map/all_to_all | solution.py:97
  226.8 2.3 fusion.71
  229.1 3.1 reshape_squeeze.6
  232.2 4.8 %fusion.8 = f32[4,8,128,128]{3,2,1,0:T(8,128)} fusion(f32[4,8,128,128]{3,2,1,0:T(8,128)S(1)} %reshape_squeeze.6), kind=kOutput, calls=%fused_computation.124 | convolution fusion | flops 805535744 | bytes 4194304 | tf_op jit(solution)/shard_map/...ab,af->...bf/dot_general | solution.py:62
  237.0 3.5 reshape_squeeze.7
  240.5 1.3 copy-done.4
  241.8 3.6 fusion.6
  245.5 5.3 %convolution_add_fusion = f32[4,8,128,128]{3,2,1,0:T(8,128)S(1)} fusion(f32[4,8,128,128]{3,2,1,0:T(8,128)S(1)} %copy-done.5, f32[4,8,128,128]{3,2,1,0:T(8,128)} %copy-done.4), kind=kOutput, calls=%fused_computation.15 | convolution fusion | flops 806060032 | bytes 6291456 | tf_op jit(solution)/shard_map/...ab,af->...bf/dot_general | solution.py:62
  250.8 3.6 convolution_subtract_fusion
  254.4 2.5 fusion.1
  256.9 3.5 fusion
  260.4 3.7 subtract_bitcast_fusion
  264.1 2.7 stack.67
  266.9 5.8 %add_bitcast_fusion = f32[4,8,128,128]{3,2,1,0:T(8,128)} fusion(f32[128,4,8,128]{3,0,2,1:T(8,128)} %fusion, f32[4,8,128,128]{3,2,1,0:T(8,128)S(1)} %convolution_add_fusion, f32[4,8,128,128]{3,2,1,0:T(8,128)} %copy-done.1, f32[128,128]{1,0:T(8,128)S(1)} %copy.84, f32[128,128]{1,0:T(8,128)S(1)} %copy.79), kind=kOutput, calls=%fused_computation.8 | convolution fusion | flops 807632896 | bytes 8519680 | tf_op jit(solution)/shard_map/...bf,bg->...gf/dot_general | solution.py:74
  272.6 2.8 stack.66
  275.5 2.1 maximum_multiply_fusion
  277.6 5.3 %constant_dynamic-slice_fusion = (f32[2,1,4,8,1,1024]{5,4,3,2,1,0:T(1,128)S(1)}, f32[2,1,4,8,1,1024]{5,4,3,2,1,0:T(1,128)S(1)}, f32[2,1,4,8,1,1024]{5,4,3,2,1,0:...) fusion(f32[2,1,4,8,16,1024]{5,4,3,2,1,0:T(8,128)S(1)} %maximum_, ...), kind=kLoop, calls=%fused_computation.193 | loop fusion | bytes 8388672 | tf_op jit(solution)/shard_map/dynamic-slice.15
  282.9 2.6 collective-permute-start.2
  285.6 2.6 collective-permute-start.3
  290.9 4.5 %collective-permute-done.2 = f32[2,1,4,8,1024]{4,3,2,0,1:T(8,128)S(1)} collective-permute-done((f32[2,1,4,8,1024]{4,3,2,0,1:T(8,128)S(1)}, f32[2,1,4,8,1024]{4,3,2,0,1:T(8,128)S(1)}, u32[]{:S(2)}, u32[]{:S(2)}) %collective-permute-start.2) | collective-permute-done | bytes 262176 | tf_op jit(solution)/shard_map/ppermute | solution.py:25
  296.1 10.8 %collective-permute-done.3 = f32[2,1,4,8,1024]{4,3,2,0,1:T(8,128)S(1)} collective-permute-done((f32[2,1,4,8,1024]{4,3,2,0,1:T(8,128)S(1)}, f32[2,1,4,8,1024]{4,3,2,0,1:T(8,128)S(1)}, u32[]{:S(2)}, u32[]{:S(2)}) %collective-permute-start.3) | collective-permute-done | bytes 262176 | tf_op jit(solution)/shard_map/ppermute | solution.py:25
  307.7 1.5 collective-permute-start.9
  309.9 19.1 %collective-permute-start.10 = (f32[2,1,4,8,1024]{4,3,2,0,1:T(8,128)S(1)}, f32[2,1,4,8,1024]{4,3,2,0,1:T(8,128)S(1)}, u32[]{:S(2)}, u32[]{:S(2)}) collective-permute-start(f32[2,1,4,8,1024]{4,3,2,0,1:T(8,128)S(1)} %bitcast.276), channel_id=1, source_target_pairs={{0,17},{1,16},{2,19},{3,18},{8,25},{9,24},{10,27},{11,26},{16,1},{... | collective-permute-start | bytes 786440 | tf_op jit(solution)/shard_map/ppermute | solution.py:25
  331.0 2.8 collective-permute-start.12
  336.2 11.4 %collective-permute-start.14 = (f32[2,1,4,8,1024]{4,3,2,0,1:T(8,128)S(1)}, f32[2,1,4,8,1024]{4,3,2,0,1:T(8,128)S(1)}, u32[]{:S(2)}, u32[]{:S(2)}) collective-permute-start(f32[2,1,4,8,1024]{4,3,2,0,1:T(8,128)S(1)} %bitcast.272), channel_id=1, source_target_pairs={{0,25},{1,24},{2,27},{3,26},{8,17},{9,16},{10,19},{11,18},{16,9},{... | collective-permute-start | bytes 786440 | tf_op jit(solution)/shard_map/ppermute | solution.py:25
  349.5 3.0 collective-permute-done.11
  354.0 7.7 %collective-permute-done.13 = f32[2,1,4,8,1024]{4,3,2,0,1:T(8,128)S(1)} collective-permute-done((f32[2,1,4,8,1024]{4,3,2,0,1:T(8,128)S(1)}, f32[2,1,4,8,1024]{4,3,2,0,1:T(8,128)S(1)}, u32[]{:S(2)}, u32[]{:S(2)}) %collective-permute-start.13) | collective-permute-done | bytes 262176 | tf_op jit(solution)/shard_map/ppermute | solution.py:25
  364.6 7.7 %collective-permute-done.16 = f32[2,1,4,8,1024]{4,3,2,0,1:T(8,128)S(1)} collective-permute-done((f32[2,1,4,8,1024]{4,3,2,0,1:T(8,128)S(1)}, f32[2,1,4,8,1024]{4,3,2,0,1:T(8,128)S(1)}, u32[]{:S(2)}, u32[]{:S(2)}) %collective-permute-start.16) | collective-permute-done | bytes 262176 | tf_op jit(solution)/shard_map/ppermute | solution.py:25
  373.0 4.9 %gather_fusion = f32[16,2,4,8,1024]{4,3,2,1,0:T(8,128)} fusion(f32[16,2,4,8,1024]{4,3,2,1,0:T(8,128)} %bitcast.32, s32[1024]{0:T(1024)S(1)} %pad_clamp_fusion), kind=kCustom, calls=%fused_computation | custom fusion | bytes 8388672 | tf_op jit(solution)/shard_map/gather | solution.py:26
  377.9 2.5 copy.86
  381.7 5.2 %multiply_add_fusion = f32[1,16,4,8,1024]{4,3,2,1,0:T(8,128)S(1)} fusion(f32[4,8,1024]{2,1,0:T(8,128)S(1)} %get-tuple-element.40, f32[16,1024]{1,0:T(8,128)S(1)} %get-tuple-element.125, f32[4,8,1024]{2,1,0:T(8,128)S(1)} %get-tuple-element.41, f32[16,1024]{1,0:T(8,128)S(1)} %get-tuple-element.126, f32[4,8,1024]{2,1,0:T(8,128)S(1)} %get-tuple-element.42, ...), kind=kLoop, calls=%fused_computation.5 | loop fusion | flops 33030144 | bytes 8388608 | tf_op jit(solution)/shard_map/add | solution.py:123
  387.0 5.3 %multiply_subtract_fusion = f32[1,16,4,8,1024]{4,3,2,1,0:T(8,128)S(1)} fusion(f32[4,8,1024]{2,1,0:T(8,128)S(1)} %get-tuple-element.40, f32[16,1024]{1,0:T(8,128)S(1)} %get-tuple-element.125, f32[4,8,1024]{2,1,0:T(8,128)S(1)} %get-tuple-element.41, f32[16,1024]{1,0:T(8,128)S(1)} %get-tuple-element.126, f32[4,8,1024]{2,1,0:T(8,128)S(1)} %get-tuple-element.42, ...), kind=kLoop, calls=%fused_computation.6 | loop fusion | flops 33030144 | bytes 8388608 | tf_op jit(solution)/shard_map/sub | solution.py:122
  392.3 2.3 pad_maximum_fusion.1
  (124 shorter events, 24.7 us)
Async XLA Ops:
  6.5 12.8 %copy-start.7 = (f32[2,17,16]{1,2,0:T(8,128)S(1)}, f32[2,17,16]{1,2,0:T(8,128)}, u32[]{:S(2)}) copy-start(f32[2,17,16]{1,2,0:T(8,128)} %param.5) | copy-start | bytes 6532
  6.5 168.1 %all-gather.2.cloned.1.call-start = ((), (), s32[]{:S(2)}) async-start(), calls=%async_computation.1 | async-start | bytes 3145728 | tf_op jit(solution)/shard_map/all_gather | solution.py:112
  11.2 50.1 %collective-permute-start = (f32[2,4,8,8192]{3,2,1,0:T(8,128)}, f32[2,4,8,8192]{3,2,1,0:T(8,128)}, u32[]{:S(2)}, u32[]{:S(2)}) collective-permute-start(f32[2,4,8,8192]{3,2,1,0:T(8,128)} %get-tuple-element.91), channel_id=1, source_target_pairs={{0,1},{1,2},{2,3},{4,5},{5,6},{6,7},{8,9},{9,10},{10,11},{12,13},{... | collective-permute-start | bytes 6291464 | tf_op jit(solution)/shard_map/ppermute | solution.py:37
  17.5 51.1 %collective-permute-start.1 = (f32[2,4,8,8192]{3,2,1,0:T(8,128)}, f32[2,4,8,8192]{3,2,1,0:T(8,128)}, u32[]{:S(2)}, u32[]{:S(2)}) collective-permute-start(f32[2,4,8,8192]{3,2,1,0:T(8,128)} %get-tuple-element.92), channel_id=1, source_target_pairs={{1,0},{2,1},{3,2},{5,4},{6,5},{7,6},{9,8},{10,9},{11,10},{13,12},{... | collective-permute-start | bytes 6291464 | tf_op jit(solution)/shard_map/ppermute | solution.py:38
  20.6 43.8 %copy-start = (f32[2,4,16,8192]{3,2,1,0:T(8,128)S(1)}, f32[2,4,16,8192]{3,2,1,0:T(8,128)}, u32[]{:S(2)}) copy-start(f32[2,4,16,8192]{3,2,1,0:T(8,128)} %param.4) | copy-start | bytes 12582916
  168.6 6.0 %copy-start.21 = (s32[16]{0:T(128)S(1)}, s32[16]{0:T(128)}, u32[]{:S(2)}) copy-start(s32[16]{0:T(128)} %param.7) | copy-start | bytes 196
  168.6 52.8 %all-to-all-start = ((f32[2,4,16,8192]{3,1,0,2:T(4,128)}), f32[2,4,16,8192]{3,1,0,2:T(4,128)}, u32[]{:S(2)}, u32[]{:S(2)}) async-start(f32[2,4,16,8192]{3,1,0,2:T(4,128)} %copy.73), calls=%async_computation | async-start | bytes 8388608 | tf_op jit(solution)/shard_map/all_to_all | solution.py:97
  232.2 4.9 %copy-start.2 = (f32[4,8,128,128]{3,2,1,0:T(8,128)}, f32[4,8,128,128]{3,2,1,0:T(8,128)S(1)}, u32[]{:S(2)}) copy-start(f32[4,8,128,128]{3,2,1,0:T(8,128)S(1)} %reshape_squeeze.6) | copy-start | bytes 6291460
  240.5 1.3 copy-start.4
  241.8 3.6 copy-start.5
  245.5 5.3 %copy-start.3 = (f32[4,8,128,128]{3,2,1,0:T(8,128)S(1)}, f32[4,8,128,128]{3,2,1,0:T(8,128)}, u32[]{:S(2)}) copy-start(f32[4,8,128,128]{3,2,1,0:T(8,128)} %copy-done.2) | copy-start | bytes 6291460
  254.4 6.0 %copy-start.1 = (f32[4,8,128,128]{3,2,1,0:T(8,128)}, f32[4,8,128,128]{3,2,1,0:T(8,128)S(1)}, u32[]{:S(2)}) copy-start(f32[4,8,128,128]{3,2,1,0:T(8,128)S(1)} %convolution_subtract_fusion) | copy-start | bytes 6291460
  272.6 2.8 copy-start.6
  277.6 7.9 %copy-start.19 = (f32[1,16,1,1024]{3,2,1,0:T(1,128)S(1)}, f32[1,16,1,1024]{3,2,1,0:T(1,128)}, u32[]{:S(2)}) copy-start(f32[1,16,1,1024]{3,2,1,0:T(1,128)} %get-tuple-element.93) | copy-start | bytes 196612
  277.6 7.9 %copy-start.20 = (f32[1,16,1,1024]{3,2,1,0:T(1,128)S(1)}, f32[1,16,1,1024]{3,2,1,0:T(1,128)}, u32[]{:S(2)}) copy-start(f32[1,16,1,1024]{3,2,1,0:T(1,128)} %get-tuple-element.112) | copy-start | bytes 196612
  282.9 12.5 %collective-permute-start.2 = (f32[2,1,4,8,1024]{4,3,2,0,1:T(8,128)S(1)}, f32[2,1,4,8,1024]{4,3,2,0,1:T(8,128)S(1)}, u32[]{:S(2)}, u32[]{:S(2)}) collective-permute-start(f32[2,1,4,8,1024]{4,3,2,0,1:T(8,128)S(1)} %bitcast.283), channel_id=1, source_target_pairs={{0,1},{1,0},{2,3},{3,2},{8,9},{9,8},{10,11},{11,10},{16,17},{17,16... | collective-permute-start | bytes 786440 | tf_op jit(solution)/shard_map/ppermute | solution.py:25
  285.6 21.4 %collective-permute-start.3 = (f32[2,1,4,8,1024]{4,3,2,0,1:T(8,128)S(1)}, f32[2,1,4,8,1024]{4,3,2,0,1:T(8,128)S(1)}, u32[]{:S(2)}, u32[]{:S(2)}) collective-permute-start(f32[2,1,4,8,1024]{4,3,2,0,1:T(8,128)S(1)} %bitcast.284), channel_id=1, source_target_pairs={{0,2},{1,3},{2,0},{3,1},{8,10},{9,11},{10,8},{11,9},{16,18},{17,19... | collective-permute-start | bytes 786440 | tf_op jit(solution)/shard_map/ppermute | solution.py:25
  289.0 18.6 %collective-permute-start.4 = (f32[2,1,4,8,1024]{4,3,2,0,1:T(8,128)S(1)}, f32[2,1,4,8,1024]{4,3,2,0,1:T(8,128)S(1)}, u32[]{:S(2)}, u32[]{:S(2)}) collective-permute-start(f32[2,1,4,8,1024]{4,3,2,0,1:T(8,128)S(1)} %bitcast.282), channel_id=1, source_target_pairs={{0,3},{1,2},{2,1},{3,0},{8,11},{9,10},{10,9},{11,8},{16,19},{17,18... | collective-permute-start | bytes 786440 | tf_op jit(solution)/shard_map/ppermute | solution.py:25
  289.2 20.7 %collective-permute-start.5 = (f32[2,1,4,8,1024]{4,3,2,0,1:T(8,128)S(1)}, f32[2,1,4,8,1024]{4,3,2,0,1:T(8,128)S(1)}, u32[]{:S(2)}, u32[]{:S(2)}) collective-permute-start(f32[2,1,4,8,1024]{4,3,2,0,1:T(8,128)S(1)} %bitcast.281), channel_id=1, source_target_pairs={{0,8},{1,9},{2,10},{3,11},{8,0},{9,1},{10,2},{11,3},{16,24},{17,25... | collective-permute-start | bytes 786440 | tf_op jit(solution)/shard_map/ppermute | solution.py:25
  289.3 40.5 %collective-permute-start.6 = (f32[2,1,4,8,1024]{4,3,2,0,1:T(8,128)S(1)}, f32[2,1,4,8,1024]{4,3,2,0,1:T(8,128)S(1)}, u32[]{:S(2)}, u32[]{:S(2)}) collective-permute-start(f32[2,1,4,8,1024]{4,3,2,0,1:T(8,128)S(1)} %bitcast.280), channel_id=1, source_target_pairs={{0,9},{1,8},{2,11},{3,10},{8,1},{9,0},{10,3},{11,2},{16,25},{17,24... | collective-permute-start | bytes 786440 | tf_op jit(solution)/shard_map/ppermute | solution.py:25
  295.4 35.6 %collective-permute-start.7 = (f32[2,1,4,8,1024]{4,3,2,0,1:T(8,128)S(1)}, f32[2,1,4,8,1024]{4,3,2,0,1:T(8,128)S(1)}, u32[]{:S(2)}, u32[]{:S(2)}) collective-permute-start(f32[2,1,4,8,1024]{4,3,2,0,1:T(8,128)S(1)} %bitcast.279), channel_id=1, source_target_pairs={{0,10},{1,11},{2,8},{3,9},{8,2},{9,3},{10,0},{11,1},{16,26},{17,27... | collective-permute-start | bytes 786440 | tf_op jit(solution)/shard_map/ppermute | solution.py:25
  307.0 27.5 %collective-permute-start.8 = (f32[2,1,4,8,1024]{4,3,2,0,1:T(8,128)S(1)}, f32[2,1,4,8,1024]{4,3,2,0,1:T(8,128)S(1)}, u32[]{:S(2)}, u32[]{:S(2)}) collective-permute-start(f32[2,1,4,8,1024]{4,3,2,0,1:T(8,128)S(1)} %bitcast.278), channel_id=1, source_target_pairs={{0,11},{1,10},{2,9},{3,8},{8,3},{9,2},{10,1},{11,0},{16,27},{17,26... | collective-permute-start | bytes 786440 | tf_op jit(solution)/shard_map/ppermute | solution.py:25
  307.7 28.5 %collective-permute-start.9 = (f32[2,1,4,8,1024]{4,3,2,0,1:T(8,128)S(1)}, f32[2,1,4,8,1024]{4,3,2,0,1:T(8,128)S(1)}, u32[]{:S(2)}, u32[]{:S(2)}) collective-permute-start(f32[2,1,4,8,1024]{4,3,2,0,1:T(8,128)S(1)} %bitcast.277), channel_id=1, source_target_pairs={{0,16},{1,17},{2,18},{3,19},{8,24},{9,25},{10,26},{11,27},{16,0},{... | collective-permute-start | bytes 786440 | tf_op jit(solution)/shard_map/ppermute | solution.py:25
  309.9 38.4 %collective-permute-start.10 = (f32[2,1,4,8,1024]{4,3,2,0,1:T(8,128)S(1)}, f32[2,1,4,8,1024]{4,3,2,0,1:T(8,128)S(1)}, u32[]{:S(2)}, u32[]{:S(2)}) collective-permute-start(f32[2,1,4,8,1024]{4,3,2,0,1:T(8,128)S(1)} %bitcast.276), channel_id=1, source_target_pairs={{0,17},{1,16},{2,19},{3,18},{8,25},{9,24},{10,27},{11,26},{16,1},{... | collective-permute-start | bytes 786440 | tf_op jit(solution)/shard_map/ppermute | solution.py:25
  329.8 22.7 %collective-permute-start.11 = (f32[2,1,4,8,1024]{4,3,2,0,1:T(8,128)S(1)}, f32[2,1,4,8,1024]{4,3,2,0,1:T(8,128)S(1)}, u32[]{:S(2)}, u32[]{:S(2)}) collective-permute-start(f32[2,1,4,8,1024]{4,3,2,0,1:T(8,128)S(1)} %bitcast.275), channel_id=1, source_target_pairs={{0,18},{1,19},{2,16},{3,17},{8,26},{9,27},{10,24},{11,25},{16,2},{... | collective-permute-start | bytes 786440 | tf_op jit(solution)/shard_map/ppermute | solution.py:25
  331.0 22.3 %collective-permute-start.12 = (f32[2,1,4,8,1024]{4,3,2,0,1:T(8,128)S(1)}, f32[2,1,4,8,1024]{4,3,2,0,1:T(8,128)S(1)}, u32[]{:S(2)}, u32[]{:S(2)}) collective-permute-start(f32[2,1,4,8,1024]{4,3,2,0,1:T(8,128)S(1)} %bitcast.274), channel_id=1, source_target_pairs={{0,19},{1,18},{2,17},{3,16},{8,27},{9,26},{10,25},{11,24},{16,3},{... | collective-permute-start | bytes 786440 | tf_op jit(solution)/shard_map/ppermute | solution.py:25
  334.5 27.3 %collective-permute-start.13 = (f32[2,1,4,8,1024]{4,3,2,0,1:T(8,128)S(1)}, f32[2,1,4,8,1024]{4,3,2,0,1:T(8,128)S(1)}, u32[]{:S(2)}, u32[]{:S(2)}) collective-permute-start(f32[2,1,4,8,1024]{4,3,2,0,1:T(8,128)S(1)} %bitcast.273), channel_id=1, source_target_pairs={{0,24},{1,25},{2,26},{3,27},{8,16},{9,17},{10,18},{11,19},{16,8},{... | collective-permute-start | bytes 786440 | tf_op jit(solution)/shard_map/ppermute | solution.py:25
  336.2 26.3 %collective-permute-start.14 = (f32[2,1,4,8,1024]{4,3,2,0,1:T(8,128)S(1)}, f32[2,1,4,8,1024]{4,3,2,0,1:T(8,128)S(1)}, u32[]{:S(2)}, u32[]{:S(2)}) collective-permute-start(f32[2,1,4,8,1024]{4,3,2,0,1:T(8,128)S(1)} %bitcast.272), channel_id=1, source_target_pairs={{0,25},{1,24},{2,27},{3,26},{8,17},{9,16},{10,19},{11,18},{16,9},{... | collective-permute-start | bytes 786440 | tf_op jit(solution)/shard_map/ppermute | solution.py:25
  348.3 15.5 %collective-permute-start.15 = (f32[2,1,4,8,1024]{4,3,2,0,1:T(8,128)S(1)}, f32[2,1,4,8,1024]{4,3,2,0,1:T(8,128)S(1)}, u32[]{:S(2)}, u32[]{:S(2)}) collective-permute-start(f32[2,1,4,8,1024]{4,3,2,0,1:T(8,128)S(1)} %bitcast.271), channel_id=1, source_target_pairs={{0,26},{1,27},{2,24},{3,25},{8,18},{9,19},{10,16},{11,17},{16,10},... | collective-permute-start | bytes 786440 | tf_op jit(solution)/shard_map/ppermute | solution.py:25
  352.5 19.8 %collective-permute-start.16 = (f32[2,1,4,8,1024]{4,3,2,0,1:T(8,128)S(1)}, f32[2,1,4,8,1024]{4,3,2,0,1:T(8,128)S(1)}, u32[]{:S(2)}, u32[]{:S(2)}) collective-permute-start(f32[2,1,4,8,1024]{4,3,2,0,1:T(8,128)S(1)} %bitcast.270), channel_id=1, source_target_pairs={{0,27},{1,26},{2,25},{3,24},{8,19},{9,18},{10,17},{11,16},{16,11},... | collective-permute-start | bytes 786440 | tf_op jit(solution)/shard_map/ppermute | solution.py:25
  380.6 0.8 copy-start.8
  380.6 0.9 copy-start.9
  380.6 0.9 copy-start.10
  380.6 0.9 copy-start.11
  380.6 0.9 copy-start.12
  380.6 1.0 copy-start.13
  380.6 1.0 copy-start.14
  380.6 1.0 copy-start.15
  380.7 1.0 copy-start.16
  380.7 1.0 copy-start.17
  380.7 1.1 copy-start.18
Sparse Core Ops, SparseCore 0:
  18.9 35.4 all-gather.1
